TPU v7x, 32 devices: a whole 2x2x4 slice. The times are simulated.
32 devices in a mesh: dp: 4 (over x, core), expert: 8 (over z, y).
Axes of the slice: x: 2, y: 2, z: 4, core: 2. Of those that a mesh axis runs over, the one named last changes fastest.
Arguments:
- tokens: bfloat16 [4096, 4096], P(('dp', 'expert')), may hold values from -6 to 6
- moe_gain: float32 [4096], replicated, may hold values from 0.5 to 1.5
- route_ids: int32 [4096, 2], P(('dp', 'expert')), may hold values from 0 to 7, all different within a row; in each aligned block of 128 rows (0 to 127, 128 to 255, ...) at most 40 rows name the same one
- route_gates: float32 [4096, 2], P(('dp', 'expert')), may hold values from 0.1 to 1
- gate_halves: bfloat16 [32, 4096, 384], P(('dp', 'expert')), may hold values from -0.09375 to 0.09375
- up_halves: bfloat16 [32, 4096, 384], P(('dp', 'expert')), may hold values from -0.09375 to 0.09375
- down_halves: bfloat16 [32, 384, 4096], P(('dp', 'expert')), may hold values from -0.15625 to 0.15625
- head_gain: float32 [4096], replicated, may hold values from 0.5 to 1.5
- head_weight: bfloat16 [4096, 512], P('expert'), may hold values from -0.09375 to 0.09375
- query_scale: float32 [512], replicated, may hold values from 1 to 4
- members: int32 [4096], P(('dp', 'expert')), may hold values from 0 to 4095, as said below
- click_targets: int32 [64, 8], P(('dp', 'expert')), may hold values from 0 to 55
Outputs:
- layer_out: bfloat16 [4096, 4096], P(('dp', 'expert'))
- click_logits: float32 [64, 8, 56], P(('dp', 'expert'))
- click_loss: float32 [64, 8], P(('dp', 'expert'))
Inputs may be any that keep to these rules, and one draw needn't show every extreme that they name: `route_ids`: in the 128 rows of one device no expert id is named by more than 40 routes, a bound that some block reaches; the 2 ids of a row differ. `members`: for each index of dp, the 1024 entries of that dp index are a permutation of the tokens of that dp index; every device's 128 entries name exactly 16 tokens of each device of its dp index.
All inputs are finite; a program needn't handle non-finite values.
Results may differ from a plain program's by a relative error of at most 0.0081.
Values may be sent and summed in bfloat16 or wider, within the bound.
A program may use at most 192 MiB of HBM per device.

v0:
```python
import math

import jax
import jax.numpy as jnp
from jax import lax
from jax.sharding import PartitionSpec as P

PATCHES = 56
QUERIES = 8


def rms_scale(values, gains):
    mean_square = jnp.mean(values * values, axis=-1, keepdims=True)
    return values * lax.rsqrt(mean_square + 1e-06) * gains


def expert_ffn(block_in, gate_part, up_part, down_part):
    block_shape = block_in.shape
    flat_rows = block_in.reshape(-1, block_shape[-1])
    gate_out = jnp.dot(flat_rows, gate_part, preferred_element_type=jnp.float32)
    up_out = jnp.dot(flat_rows, up_part, preferred_element_type=jnp.float32)
    hidden = (jax.nn.silu(gate_out) * up_out).astype(jnp.bfloat16)
    partial_out = jnp.dot(hidden, down_part, preferred_element_type=jnp.float32).astype(
        jnp.bfloat16
    )
    return partial_out.reshape(block_shape)


def pair_sum(block_in, per_row):
    leading = block_in.shape[0]
    split_view = block_in.reshape(leading, per_row, 4, block_in.shape[2], block_in.shape[3]).astype(
        jnp.float32
    )
    return jnp.sum(split_view, axis=2).astype(jnp.bfloat16)


def shards(
    tokens,
    moe_gain,
    route_ids,
    route_gates,
    gate_halves,
    up_halves,
    down_halves,
    head_gain,
    head_weight,
    query_scale,
    members,
    click_targets,
):
    row_count = lax.axis_size("dp")
    col_count = lax.axis_size("expert")
    tok_count, model_width = tokens.shape
    route_count = route_ids.shape[1]
    expert_count = row_count * col_count // 4
    per_row = col_count // 4
    capacity = max(2, 5 * tok_count * route_count // (4 * expert_count))
    head_width = head_weight.shape[1]
    gate_part = gate_halves[0]
    up_part = up_halves[0]
    down_part = down_halves[0]
    normed = rms_scale(tokens.astype(jnp.float32), moe_gain).astype(jnp.bfloat16)
    flat_ids = route_ids.reshape(-1)
    onehot = (flat_ids[:, None] == jnp.arange(expert_count, dtype=jnp.int32)[None, :]).astype(
        jnp.int32
    )
    earlier = jnp.cumsum(onehot, axis=0) - onehot
    slot_ids = jnp.sum(earlier * onehot, axis=1)
    target = flat_ids * capacity + slot_ids
    repeated = jnp.repeat(normed, route_count, axis=0)
    dispatch = (
        jnp.zeros((expert_count * capacity, model_width), jnp.bfloat16).at[target].set(repeated)
    )
    dispatch = dispatch.reshape(row_count, per_row, capacity, model_width)
    arrived = lax.all_to_all(dispatch, "dp", split_axis=0, concat_axis=0, tiled=True)
    copies = jnp.repeat(arrived, 4, axis=1)
    partial_out = expert_ffn(
        lax.all_to_all(copies, "expert", split_axis=1, concat_axis=1, tiled=True),
        gate_part,
        up_part,
        down_part,
    )
    returned = lax.all_to_all(partial_out, "expert", split_axis=1, concat_axis=1, tiled=True)
    merged = pair_sum(returned, per_row)
    combined = lax.all_to_all(merged, "dp", split_axis=0, concat_axis=0, tiled=True)
    outputs = combined.reshape(expert_count * capacity, model_width)
    picked = outputs[target].astype(jnp.float32).reshape(tok_count, route_count, model_width)
    layer_out = (
        tokens.astype(jnp.float32) + jnp.sum(route_gates[:, :, None] * picked, axis=1)
    ).astype(jnp.bfloat16)
    head_in = rms_scale(layer_out.astype(jnp.float32), head_gain).astype(jnp.bfloat16)
    embedding = jnp.dot(
        head_in,
        lax.all_gather(head_weight, "expert", axis=0, tiled=True),
        preferred_element_type=jnp.float32,
    ).astype(jnp.bfloat16)
    row_length = col_count * tok_count
    local_ids = members % row_length
    portion = lax.all_gather(embedding, "expert", axis=0, tiled=True)
    select = (local_ids[:, None] == jnp.arange(portion.shape[0], dtype=jnp.int32)[None, :]).astype(
        jnp.bfloat16
    )
    regrouped = jnp.dot(select, portion, preferred_element_type=jnp.float32)
    span_rows = PATCHES + QUERIES
    grouped = regrouped.reshape(tok_count // span_rows, span_rows, head_width)
    key_rows = grouped[:, :PATCHES]
    query_rows = grouped[:, PATCHES:] * query_scale
    click_logits = jnp.einsum(
        "sqd,spd->sqp", query_rows, key_rows, precision=lax.Precision.HIGHEST
    ) / math.sqrt(head_width)
    log_total = jnp.log(jnp.sum(jnp.exp(click_logits), axis=-1))
    chosen_logit = jnp.take_along_axis(click_logits, click_targets[:, :, None], axis=-1)[:, :, 0]
    click_loss = log_total - chosen_logit
    return (layer_out, click_logits, click_loss)


def solution(mesh):
    in_specs = (
        P(("dp", "expert"), None),
        P(),
        P(("dp", "expert"), None),
        P(("dp", "expert"), None),
        P(("dp", "expert"), None, None),
        P(("dp", "expert"), None, None),
        P(("dp", "expert"), None, None),
        P(),
        P("expert", None),
        P(),
        P(("dp", "expert")),
        P(("dp", "expert"), None),
    )
    out_specs = (
        P(("dp", "expert"), None),
        P(("dp", "expert"), None, None),
        P(("dp", "expert"), None),
    )
    return jax.shard_map(shards, mesh=mesh, in_specs=in_specs, out_specs=out_specs, check_vma=False)
```

profile of v0, /device:TPU:0, one launch (start us, length us, event | category | flops | bytes accessed | tf_op | source)
XLA Modules:
  0.0 750.4 jit_solution(6766608364450244354)
XLA Ops:
  7.2 0.0 copy-start
  7.2 0.9 copy.42
  8.1 0.1 eq.44
  8.3 0.1 eq.40
  8.4 0.7 broadcast_multiply_fusion
  9.1 0.6 reduce-window.6
  9.7 0.2 slice_reduce_fusion
  9.9 0.1 copy.41
  10.0 0.1 mul.83
  10.2 1.5 fusion.12
  11.7 1.6 fusion.14
  13.3 3.5 broadcast_in_dim.7
  16.8 4.1 reshape.154
  20.9 0.1 fusion.32
  21.0 6.3 scatter_custom_fusion
  27.2 35.6 %all_to_all.20 = bf16[4,2,40,4096]{3,2,1,0:T(8,128)(2,1)S(1)} all-to-all(bf16[4,2,40,4096]{3,2,1,0:T(8,128)(2,1)} %bitcast.46), channel_id=1, replica_groups=mesh['dp'=4,'expert'=8] {'dp'}, dimensions={0} | all-to-all | bytes 5242880 | tf_op jit(solution)/shard_map/all_to_all | solution.py:75
  62.8 1.8 copy.44
  64.6 7.1 broadcast_in_dim.8
  71.7 234.9 %all_to_all.21 = bf16[4,8,40,4096]{3,2,0,1:T(8,128)(2,1)} all-to-all(bf16[4,8,40,4096]{3,2,0,1:T(8,128)(2,1)} %bitcast.42), channel_id=1, replica_groups=mesh['dp'=4,'expert'=8] {'expert'}, dimensions={1} | all-to-all | bytes 20971520 | tf_op jit(solution)/shard_map/all_to_all | solution.py:78
  306.6 9.6 %copy.45 = bf16[4,8,40,4096]{3,2,1,0:T(8,128)(2,1)} copy(bf16[4,8,40,4096]{3,2,0,1:T(8,128)(2,1)} %all_to_all.21) | data formatting | bytes 20971520 | tf_op jit(solution)/shard_map/all_to_all | solution.py:78
  316.2 10.2 %fusion.2 = f32[1280,384]{1,0:T(8,128)} fusion(bf16[1280,4096]{1,0:T(8,128)(2,1)} %bitcast.43, bf16[1,4096,384]{2,1,0:T(8,128)(2,1)} %param.16), kind=kOutput, calls=%fused_computation.9 | convolution fusion | flops 4026531840 | bytes 15597568 | tf_op jit(solution)/shard_map/dot_general | solution.py:20
  326.4 0.0 copy-done
  326.4 17.2 %convolution_convert_fusion = bf16[1280,4096]{1,0:T(8,128)(2,1)} fusion(bf16[1,384,4096]{2,1,0:T(8,128)(2,1)S(1)} %copy-done, bf16[1280,4096]{1,0:T(8,128)(2,1)} %bitcast.44, bf16[1,4096,384]{2,1,0:T(8,128)(2,1)} %param.17, f32[1280,384]{1,0:T(8,128)} %fusion.2), kind=kOutput, calls=%fused_computation.3 | convolution fusion | flops 8061255680 | bytes 29229056 | tf_op jit(solution)/shard_map/dot_general | solution.py:23
  343.6 9.6 %copy.46 = bf16[4,8,40,4096]{3,2,0,1:T(8,128)(2,1)} copy(bf16[4,8,40,4096]{3,2,1,0:T(8,128)(2,1)} %bitcast.45) | data formatting | bytes 20971520 | tf_op jit(solution)/shard_map/reshape | solution.py:26
  353.2 5.2 all-to-all-start.2
  358.3 0.0 all-gather.3.cloned.1.call-start
  358.4 0.7 all-gather.3.cloned.1.call-update
  359.1 276.9 %all-to-all-done.2 = bf16[4,8,40,4096]{3,2,0,1:T(8,128)(2,1)} async-done(((bf16[4,8,40,4096]{3,2,0,1:T(8,128)(2,1)}), bf16[4,8,40,4096]{3,2,0,1:T(8,128)(2,1)}, u32[]{:S(2)}, u32[]{:S(2)}) %all-to-all-start.2) | async-done | bytes 10485792 | tf_op jit(solution)/shard_map/all_to_all | solution.py:83
  635.9 6.2 bitcast_reduce_fusion
  642.2 1.8 copy.47
  644.0 0.0 copy-start.6
  644.0 3.8 all-to-all-start.3
  647.8 0.3 all-gather.5.cloned.1.call-start
  648.1 0.0 copy-done.6
  648.1 0.1 copy.40
  648.2 30.9 %all-to-all-done.3 = bf16[4,2,40,4096]{3,2,1,0:T(8,128)(2,1)S(1)} async-done(((bf16[4,2,40,4096]{3,2,1,0:T(8,128)(2,1)}), bf16[4,2,40,4096]{3,2,1,0:T(8,128)(2,1)S(1)}, u32[]{:S(2)}, u32[]{:S(2)}) %all-to-all-start.3) | async-done | bytes 2621472 | tf_op jit(solution)/shard_map/all_to_all | solution.py:85
  679.0 3.2 gather_fusion
  682.2 5.4 reshape.133
  687.6 0.0 copy-start.3
  687.7 8.6 %multiply_reduce_fusion = f32[128,4096]{1,0:T(8,128)S(1)} fusion(f32[128,2,4096]{2,1,0:T(2,128)} %reshape.133, f32[128,2]{1,0:T(8,128)S(1)} %copy.40), kind=kLoop, calls=%fused_computation.5 | loop fusion | flops 1572864 | bytes 6292480 | tf_op jit(solution)/shard_map/reduce_sum | solution.py:89
  696.3 0.0 copy-done.3
  696.3 0.0 copy-start.7
  696.3 1.3 fusion.9
  697.6 0.0 all-gather.3.cloned.1.call-done
  697.6 0.0 copy-done.7
  697.6 0.0 copy-start.4
  697.6 0.0 copy-start.8
  697.7 0.0 copy-start.5
  697.7 0.0 copy-start.1
  697.7 4.1 convolution_convert_fusion.1
  701.7 0.0 all-gather.5.cloned.1.call-update
  701.8 0.0 copy-done.4
  701.8 0.1 reshape.144
  701.9 0.0 copy-done.8
  701.9 38.3 %all-gather.5.cloned.1.call-done = bf16[1024,512]{1,0:T(8,128)(2,1)} async-done(((bf16[128,512]{1,0:T(8,128)(2,1)}), bf16[1024,512]{1,0:T(8,128)(2,1)}) %all-gather.5.cloned.1.call-update) | async-done | bytes 1048592 | tf_op jit(solution)/shard_map/all_gather | solution.py:99
  740.3 1.6 fusion.27
  741.8 0.0 copy-done.5
  741.9 0.4 exponential_reduce_fusion
  742.2 0.0 copy-start.2
  742.2 0.7 gather_fusion.1
  742.9 0.1 gather.11
  743.0 0.6 fusion.34
  743.6 0.0 copy-done.2
  743.6 0.0 copy-done.1
  (13 shorter events, 0.1 us)
Async XLA Ops:
  7.2 319.2 %copy-start = (bf16[1,384,4096]{2,1,0:T(8,128)(2,1)S(1)}, bf16[1,384,4096]{2,1,0:T(8,128)(2,1)}, u32[]{:S(2)}) copy-start(bf16[1,384,4096]{2,1,0:T(8,128)(2,1)} %param.18) | copy-start | bytes 9437188
  353.2 282.8 %all-to-all-start.2 = ((bf16[4,8,40,4096]{3,2,0,1:T(8,128)(2,1)}), bf16[4,8,40,4096]{3,2,0,1:T(8,128)(2,1)}, u32[]{:S(2)}, u32[]{:S(2)}) async-start(bf16[4,8,40,4096]{3,2,0,1:T(8,128)(2,1)} %copy.46), calls=%async_computation.2 | async-start | bytes 20971520 | tf_op jit(solution)/shard_map/all_to_all | solution.py:83
  358.3 339.3 %all-gather.3.cloned.1.call-start = ((), (), s32[]{:S(2)}) async-start(), calls=%async_computation.4 | async-start | bytes 4718592 | tf_op jit(solution)/shard_map/all_gather | solution.py:94
  644.0 4.1 copy-start.6
  644.0 35.0 %all-to-all-start.3 = ((bf16[4,2,40,4096]{3,2,1,0:T(8,128)(2,1)}), bf16[4,2,40,4096]{3,2,1,0:T(8,128)(2,1)S(1)}, u32[]{:S(2)}, u32[]{:S(2)}) async-start(bf16[4,2,40,4096]{3,2,1,0:T(8,128)(2,1)} %copy.47), calls=%async_computation.3 | async-start | bytes 5242880 | tf_op jit(solution)/shard_map/all_to_all | solution.py:85
  647.8 92.5 %all-gather.5.cloned.1.call-start = ((), (), s32[]{:S(2)}) async-start(), calls=%async_computation.5 | async-start | bytes 1179648 | tf_op jit(solution)/shard_map/all_gather | solution.py:99
  687.6 8.6 %copy-start.3 = (bf16[128,4096]{1,0:T(8,128)(2,1)S(1)}, bf16[128,4096]{1,0:T(8,128)(2,1)}, u32[]{:S(2)}) copy-start(bf16[128,4096]{1,0:T(8,128)(2,1)} %param.12) | copy-start | bytes 3145732
  696.3 1.3 copy-start.7
  697.6 4.1 copy-start.4
  697.6 4.3 copy-start.8
  697.7 44.2 %copy-start.5 = (f32[512]{0:T(512)S(1)}, f32[512]{0:T(512)}, u32[]{:S(2)}) copy-start(f32[512]{0:T(512)} %param.21) | copy-start | bytes 6148
  697.7 45.9 %copy-start.1 = (bf16[1,384,4096]{2,1,0:T(8,128)(2,1)S(1)}, bf16[1,384,4096]{2,1,0:T(8,128)(2,1)}, u32[]{:S(2)}) copy-start(bf16[1,384,4096]{2,1,0:T(8,128)(2,1)} %param.18) | copy-start | bytes 9437188
  742.2 1.3 copy-start.2
Sparse Core Ops, SparseCore 0:
  361.3 236.6 all-gather.2
  701.9 38.3 all-gather.4
where the time goes:
time: 751 us; the launch traced here: 750 us
  waiting for transfers between devices  347 us (46%)
  blocking collectives  270 us (36%)
  local copies, waits for them, and re-layouts  55.1 us (7%)
  matrix products  33.4 us (4%)
  other arithmetic  21.3 us (3%)
  between operations  14.2 us (2%)
  starting transfers between devices  9.24 us (1%)
    all_to_all x1, waiting for transfers between devices, shards(): lax.all_to_all(partial_out, 'expert', split_axis=1, concat_axis=1, tiled=...  277 us
    all_to_all x1, blocking collectives, shards(): lax.all_to_all(copies, 'expert', split_axis=1, concat_axis=1, tiled=True)  235 us
    all_gather x1, waiting for transfers between devices, shards(): portion = lax.all_gather(embedding, 'expert', axis=0, tiled=True)  38.3 us
    all_to_all x1, blocking collectives, shards(): lax.all_to_all(dispatch, 'dp', split_axis=0, concat_axis=0, tiled=True)  35.6 us
    all_to_all x1, waiting for transfers between devices, shards(): lax.all_to_all(merged, 'dp', split_axis=0, concat_axis=0, tiled=True)  30.9 us
    dot_general x1, matrix products, expert_ffn(): jnp.dot(hidden, down_part, preferred_element_type=jnp.float32)  17.2 us
  transfers between devices with their start and end apart: 4, of which 3 were waited for; matrix products, arithmetic and copies ran while one was open for 4% of the time, Pallas kernels for 0%

commit v1 on v0

--- a/solution.py
+++ b/solution.py
@@ -1,8 +1,11 @@
+import functools
 import math
 
 import jax
 import jax.numpy as jnp
 from jax import lax
+from jax.experimental import pallas as pl
+from jax.experimental.pallas import tpu as pltpu
 from jax.sharding import PartitionSpec as P
 
 PATCHES = 56
@@ -26,12 +29,232 @@
     return partial_out.reshape(block_shape)
 
 
-def pair_sum(block_in, per_row):
-    leading = block_in.shape[0]
-    split_view = block_in.reshape(leading, per_row, 4, block_in.shape[2], block_in.shape[3]).astype(
-        jnp.float32
-    )
-    return jnp.sum(split_view, axis=2).astype(jnp.bfloat16)
+MESH = pl.DeviceIdType.MESH
+
+
+def flip(value, bits, count):
+    bit = 1
+    while bit < count:
+        if bits & bit:
+            value = value + bit * (1 - 2 * ((value // bit) % 2))
+        bit *= 2
+    return value
+
+
+def place(count, per_row):
+    dp, column = lax.axis_index("dp"), lax.axis_index("expert")
+    group, quarter = dp * per_row + column // 4, column % 4
+
+    def across(offset):
+        other = flip(group, offset, count)
+        return (other // per_row, (other % per_row) * 4 + quarter)
+
+    def beside(bits):
+        return (dp, (column // 4) * 4 + flip(quarter, bits, 4))
+
+    return group, quarter, across, beside
+
+
+def greet(count, across, beside):
+    barrier = pltpu.get_barrier_semaphore()
+    for offset in range(1, count):
+        pl.semaphore_signal(barrier, inc=1, device_id=across(offset), device_id_type=MESH)
+    for bits in (1, 2):
+        pl.semaphore_signal(barrier, inc=1, device_id=beside(bits), device_id_type=MESH)
+    pl.semaphore_wait(barrier, count + 1)
+
+
+def remote(source, target, send, receive, device):
+    return pltpu.make_async_remote_copy(
+        src_ref=source,
+        dst_ref=target,
+        send_sem=send,
+        recv_sem=receive,
+        device_id=device,
+        device_id_type=MESH,
+    )
+
+
+def via(offset):
+    return 1 + (offset // 2) % 2
+
+
+def dispatch_kernel(count, per_row, block_ref, out_ref, own, s1, r1, s2, r2, s3, r3):
+    group, quarter, across, beside = place(count, per_row)
+    greet(count, across, beside)
+    order = list(range(0, count, 2)) + list(range(1, count, 2))
+    keep = pltpu.make_async_copy(block_ref.at[group], out_ref.at[quarter, group], own.at[0])
+    started = []
+    first = {}
+    for offset in sorted(range(1, count), key=lambda o: bin(o).count("1")):
+        first[offset] = remote(
+            block_ref.at[flip(group, offset, count)],
+            out_ref.at[quarter, group],
+            s1.at[offset],
+            r1.at[offset],
+            across(offset),
+        )
+        first[offset].start()
+        started.append(first[offset])
+    keep.start()
+    second = {}
+
+    def relay(offset):
+        bits = via(offset)
+        second[bits, offset].wait_recv()
+        held = out_ref.at[flip(quarter, bits, 4), flip(group, offset, count)]
+        copy = remote(held, held, s3.at[offset], r3.at[offset], beside(3 - bits))
+        copy.start()
+        started.append(copy)
+        return copy
+
+    relays = []
+    for place_in, offset in enumerate(order):
+        slot = out_ref.at[quarter, flip(group, offset, count)]
+        if offset:
+            first[offset].wait_recv()
+        for bits in (via(offset), 3 - via(offset)):
+            second[bits, offset] = remote(
+                slot if offset else block_ref.at[group],
+                slot,
+                s2.at[bits - 1, offset],
+                r2.at[bits - 1, offset],
+                beside(bits),
+            )
+            second[bits, offset].start()
+            started.append(second[bits, offset])
+        if place_in >= 2:
+            relays.append(relay(order[place_in - 2]))
+    for offset in order[-2:]:
+        relays.append(relay(offset))
+    for offset in order:
+        second[3 - via(offset), offset].wait_recv()
+    for copy in relays:
+        copy.wait_recv()
+    for copy in started:
+        copy.wait_send()
+    keep.wait()
+
+
+def return_kernel(
+    count, per_row, part_ref, out_ref, early, merged, late, total, own, s0, r0, s1, r1, s2, r2
+):
+    group, quarter, across, beside = place(count, per_row)
+    greet(count, across, beside)
+    order = list(range(1, count, 2)) + list(range(2, count, 2)) + [0]
+    started = []
+    opening, middle, closing = {}, {}, {}
+
+    def at(bits, offset):
+        return part_ref.at[flip(quarter, bits, 4), flip(group, offset, count)]
+
+    def to_owner(bits, offset, source):
+        middle[bits, offset] = remote(
+            source,
+            late.at[bits - 1, offset],
+            s1.at[bits - 1, offset],
+            r1.at[bits - 1, offset],
+            beside(bits),
+        )
+        middle[bits, offset].start()
+        started.append(middle[bits, offset])
+
+    for offset in order:
+        bits = via(offset)
+        opening[offset] = remote(
+            at(3, offset), early.at[offset], s0.at[offset], r0.at[offset], beside(bits)
+        )
+        opening[offset].start()
+        started.append(opening[offset])
+        to_owner(bits, offset, at(bits, offset))
+    waiting = None
+    for offset in order:
+        opening[offset].wait_recv()
+        bits = 3 - via(offset)
+        merged[offset] = (
+            at(bits, offset)[...].astype(jnp.float32) + early[offset].astype(jnp.float32)
+        ).astype(jnp.bfloat16)
+        if waiting is not None:
+            to_owner(3 - via(waiting), waiting, merged.at[waiting])
+        waiting = offset
+    last_merged = waiting
+    waiting = None
+
+    def send_home(offset):
+        closing[offset] = remote(
+            total.at[offset], out_ref.at[group], s2.at[offset], r2.at[offset], across(offset)
+        )
+        closing[offset].start()
+        started.append(closing[offset])
+
+    to_owner(3 - via(last_merged), last_merged, merged.at[last_merged])
+    for offset in order:
+        for bits in (1, 2):
+            middle[bits, offset].wait_recv()
+        total[offset] = (
+            at(0, offset)[...].astype(jnp.float32)
+            + late[0, offset].astype(jnp.float32)
+            + late[1, offset].astype(jnp.float32)
+        ).astype(jnp.bfloat16)
+        if waiting is not None:
+            send_home(waiting)
+        waiting = offset
+    keep = pltpu.make_async_copy(total.at[0], out_ref.at[group], own.at[0])
+    keep.start()
+    for offset in order[:-1]:
+        closing[offset].wait_recv()
+    for copy in started:
+        copy.wait_send()
+    keep.wait()
+
+
+def dispatch_rows(blocks, per_row):
+    count, capacity, width = blocks.shape
+    dma = pltpu.SemaphoreType.DMA
+    return pl.pallas_call(
+        functools.partial(dispatch_kernel, count, per_row),
+        out_shape=jax.ShapeDtypeStruct((4, count, capacity, width), blocks.dtype),
+        in_specs=[pl.BlockSpec(memory_space=pltpu.VMEM)],
+        out_specs=pl.BlockSpec(memory_space=pl.ANY),
+        scratch_shapes=[
+            dma((1,)),
+            dma((count,)),
+            dma((count,)),
+            dma((2, count)),
+            dma((2, count)),
+            dma((count,)),
+            dma((count,)),
+        ],
+        compiler_params=pltpu.CompilerParams(collective_id=0, has_side_effects=True),
+        name="dispatch_rows",
+    )(blocks)
+
+
+def return_rows(parts, per_row):
+    _, count, capacity, width = parts.shape
+    dma = pltpu.SemaphoreType.DMA
+    block = (count, capacity, width)
+    return pl.pallas_call(
+        functools.partial(return_kernel, count, per_row),
+        out_shape=jax.ShapeDtypeStruct(block, parts.dtype),
+        in_specs=[pl.BlockSpec(memory_space=pltpu.VMEM)],
+        out_specs=pl.BlockSpec(memory_space=pl.ANY),
+        scratch_shapes=[
+            pltpu.VMEM(block, parts.dtype),
+            pltpu.VMEM(block, parts.dtype),
+            pltpu.VMEM((2, *block), parts.dtype),
+            pltpu.VMEM(block, parts.dtype),
+            dma((1,)),
+            dma((count,)),
+            dma((count,)),
+            dma((2, count)),
+            dma((2, count)),
+            dma((count,)),
+            dma((count,)),
+        ],
+        compiler_params=pltpu.CompilerParams(collective_id=1, has_side_effects=True),
+        name="return_rows",
+    )(parts)
 
 
 def shards(
@@ -66,28 +289,20 @@
     )
     earlier = jnp.cumsum(onehot, axis=0) - onehot
     slot_ids = jnp.sum(earlier * onehot, axis=1)
-    target = flat_ids * capacity + slot_ids
-    repeated = jnp.repeat(normed, route_count, axis=0)
-    dispatch = (
-        jnp.zeros((expert_count * capacity, model_width), jnp.bfloat16).at[target].set(repeated)
-    )
-    dispatch = dispatch.reshape(row_count, per_row, capacity, model_width)
-    arrived = lax.all_to_all(dispatch, "dp", split_axis=0, concat_axis=0, tiled=True)
-    copies = jnp.repeat(arrived, 4, axis=1)
-    partial_out = expert_ffn(
-        lax.all_to_all(copies, "expert", split_axis=1, concat_axis=1, tiled=True),
-        gate_part,
-        up_part,
-        down_part,
-    )
-    returned = lax.all_to_all(partial_out, "expert", split_axis=1, concat_axis=1, tiled=True)
-    merged = pair_sum(returned, per_row)
-    combined = lax.all_to_all(merged, "dp", split_axis=0, concat_axis=0, tiled=True)
-    outputs = combined.reshape(expert_count * capacity, model_width)
-    picked = outputs[target].astype(jnp.float32).reshape(tok_count, route_count, model_width)
-    layer_out = (
-        tokens.astype(jnp.float32) + jnp.sum(route_gates[:, :, None] * picked, axis=1)
-    ).astype(jnp.bfloat16)
+    target = (flat_ids * capacity + slot_ids).reshape(tok_count, route_count)
+    slots = jnp.arange(expert_count * capacity, dtype=jnp.int32)
+    chosen = target.T[:, None, :] == slots[None, :, None]
+    fill = jnp.any(chosen, axis=0).astype(jnp.bfloat16)
+    dispatch = jnp.dot(fill, normed, preferred_element_type=jnp.float32).astype(jnp.bfloat16)
+    arrived = dispatch_rows(dispatch.reshape(expert_count, capacity, model_width), per_row)
+    partial_out = expert_ffn(arrived, gate_part, up_part, down_part)
+    outputs = return_rows(partial_out, per_row).reshape(expert_count * capacity, model_width)
+    mixed = jnp.zeros((tok_count, model_width), jnp.float32)
+    for k in range(route_count):
+        pick = (target[:, k, None] == slots[None, :]).astype(jnp.bfloat16)
+        picked = jnp.dot(pick, outputs, preferred_element_type=jnp.float32)
+        mixed = mixed + route_gates[:, k, None] * picked
+    layer_out = (tokens.astype(jnp.float32) + mixed).astype(jnp.bfloat16)
     head_in = rms_scale(layer_out.astype(jnp.float32), head_gain).astype(jnp.bfloat16)
     embedding = jnp.dot(
         head_in,

time: 751 us -> 406 us (0.54)
  waiting for transfers between devices: 347 us -> 40.8 us
  Pallas kernels: 0 us -> 303 us
  blocking collectives: 270 us -> 0 us
  local copies, waits for them, and re-layouts: 55.1 us -> 2.62 us
  other arithmetic: 21.3 us -> 3.61 us
  starting transfers between devices: 9.24 us -> 0.08 us
  matrix products: 33.4 us -> 41.5 us
    all_to_all x2 -> x0, waiting for transfers between devices: 308 us -> none  [the longest x1 277 us: shards(): lax.all_to_all(partial_out, 'expert', split_axis=1, concat_axis=1, tiled=...]
    pallas_call x0 -> x2, Pallas kernels: none -> 303 us  [the longest x1 174 us: dispatch_rows(): pl.pallas_call(functools.partial(dispatch_kernel, count, per_row), out_sh...]
    all_to_all x2 -> x0, blocking collectives: 270 us -> none  [the longest x1 235 us: shards(): lax.all_to_all(copies, 'expert', split_axis=1, concat_axis=1, tiled=True)]
    reduce_sum x2 -> x0, other arithmetic: 14.9 us -> none  [the longest x1 8.63 us: shards(): jnp.sum(route_gates[:, :, None] * picked, axis=1)]
    reshape x2 -> x0, local copies, waits for them, and re-layouts: 13.7 us -> none  [the longest x1 9.61 us: expert_ffn(): return partial_out.reshape(block_shape)]
    all_to_all x2 -> x0, local copies, waits for them, and re-layouts: 11.4 us -> none  [the longest x1 9.61 us: shards(): lax.all_to_all(copies, 'expert', split_axis=1, concat_axis=1, tiled=True)]
    broadcast_in_dim x2 -> x0, local copies, waits for them, and re-layouts: 10.5 us -> none  [the longest x1 7.06 us: shards(): copies = jnp.repeat(arrived, 4, axis=1)]
    all_to_all x2 -> x0, starting transfers between devices: 8.94 us -> none  [the longest x1 5.15 us: shards(): lax.all_to_all(partial_out, 'expert', split_axis=1, concat_axis=1, tiled=...]
  transfers between devices with their start and end apart: 4 -> 2, of which waited for: 3 -> 1; matrix products, arithmetic and copies ran while one was open for 4% -> 10% of each run, Pallas kernels for 0% -> 75%
where the time goes in v1:
time: 406 us; the launch traced here: 405 us
  Pallas kernels  303 us (75%)
  matrix products  41.5 us (10%)
  waiting for transfers between devices  40.8 us (10%)
  between operations  14.2 us (3%)
    pallas_call x1, Pallas kernels, dispatch_rows(): pl.pallas_call(functools.partial(dispatch_kernel, count, per_row), out_sh...  174 us
    pallas_call x1, Pallas kernels, return_rows(): pl.pallas_call(functools.partial(return_kernel, count, per_row), out_shap...  129 us
    all_gather x1, waiting for transfers between devices, shards(): portion = lax.all_gather(embedding, 'expert', axis=0, tiled=True)  40.1 us
    dot_general x1, matrix products, expert_ffn(): jnp.dot(hidden, down_part, preferred_element_type=jnp.float32)  17.2 us
    dot_general x1, matrix products, expert_ffn(): gate_out = jnp.dot(flat_rows, gate_part, preferred_element_type=jnp.float32)  10.1 us
  transfers between devices with their start and end apart: 2, of which 1 were waited for; matrix products, arithmetic and copies ran while one was open for 10% of the time, Pallas kernels for 75%

profile of v1, /device:TPU:0, one launch (start us, length us, event | category | flops | bytes accessed | tf_op | source)
XLA Modules:
  0.0 405.3 jit_solution(12515584531681812756)
XLA Ops:
  7.2 0.0 copy-start
  7.2 0.0 all-gather.3.cloned.1.call-start
  7.2 0.7 all-gather.3.cloned.1.call-update
  7.9 0.0 all-gather.5.cloned.1.call-start
  8.0 0.9 copy.30
  8.9 0.1 eq.87
  9.0 0.1 eq.83
  9.2 0.6 reduce-window.6
  9.8 0.2 slice_reduce_fusion
  10.0 0.1 fusion.38
  10.1 0.1 reduce_sum.39
  10.3 0.1 copy.32
  10.3 0.7 multiply_add_fusion
  11.1 1.5 fusion.15
  12.6 3.7 convolution_convert_fusion.1
  16.3 173.9 %dispatch_rows.1 = bf16[4,8,40,4096]{3,2,1,0:T(8,128)(2,1)} custom-call(bf16[8,40,4096]{2,1,0:T(8,128)(2,1)} %bitcast.50), custom_call_target="tpu_custom_call" | custom-call | tf_op jit(solution)/shard_map/dispatch_rows/pallas_call | solution.py:214
  190.2 10.1 %fusion.5 = f32[1280,384]{1,0:T(8,128)} fusion(bf16[1280,4096]{1,0:T(8,128)(2,1)} %bitcast.51, bf16[1,4096,384]{2,1,0:T(8,128)(2,1)} %param.16), kind=kOutput, calls=%fused_computation.11 | convolution fusion | flops 4026531840 | bytes 15597568 | tf_op jit(solution)/shard_map/dot_general | solution.py:23
  200.4 0.0 copy-done
  200.4 17.2 %convolution_convert_fusion = bf16[1280,4096]{1,0:T(8,128)(2,1)} fusion(bf16[1,384,4096]{2,1,0:T(8,128)(2,1)S(1)} %copy-done, bf16[1280,4096]{1,0:T(8,128)(2,1)} %bitcast.52, bf16[1,4096,384]{2,1,0:T(8,128)(2,1)} %param.17, f32[1280,384]{1,0:T(8,128)} %fusion.5), kind=kOutput, calls=%fused_computation.1 | convolution fusion | flops 8061255680 | bytes 29229056 | tf_op jit(solution)/shard_map/dot_general | solution.py:26
  217.6 0.0 copy-start.6
  217.6 128.6 %return_rows.1 = bf16[8,40,4096]{2,1,0:T(8,128)(2,1)} custom-call(bf16[4,8,40,4096]{3,2,1,0:T(8,128)(2,1)} %bitcast.53), custom_call_target="tpu_custom_call" | custom-call | tf_op jit(solution)/shard_map/return_rows/pallas_call | solution.py:237
  346.2 0.0 copy-start.2
  346.2 0.0 copy-start.3
  346.2 0.0 copy-done.6
  346.3 2.6 convolution_multiply_fusion.1
  348.9 0.0 copy-done.2
  348.9 0.1 copy-done.3
  349.0 0.0 copy-start.7
  349.0 2.0 fusion.12
  351.0 0.0 all-gather.3.cloned.1.call-done
  351.0 0.0 copy-done.7
  351.0 0.0 copy-start.4
  351.0 0.0 copy-start.8
  351.0 0.0 copy-start.5
  351.0 3.9 convolution_convert_fusion.2
  355.0 0.0 all-gather.5.cloned.1.call-update
  355.0 0.0 copy-done.4
  355.1 0.1 reshape.93
  355.1 0.0 copy-done.8
  355.2 40.1 %all-gather.5.cloned.1.call-done = bf16[1024,512]{1,0:T(8,128)(2,1)} async-done(((bf16[128,512]{1,0:T(8,128)(2,1)}), bf16[1024,512]{1,0:T(8,128)(2,1)}) %all-gather.5.cloned.1.call-update) | async-done | bytes 1048592 | tf_op jit(solution)/shard_map/all_gather | solution.py:314
  395.2 1.6 fusion.30
  396.8 0.0 copy-done.5
  396.8 0.4 exponential_reduce_fusion
  397.2 0.0 copy-start.1
  397.2 0.7 gather_fusion
  397.8 0.1 gather.7
  397.9 0.6 fusion.40
  398.5 0.0 copy-done.1
  (14 shorter events, 0.1 us)
Async XLA Ops:
  7.2 193.2 %copy-start = (bf16[1,384,4096]{2,1,0:T(8,128)(2,1)S(1)}, bf16[1,384,4096]{2,1,0:T(8,128)(2,1)}, u32[]{:S(2)}) copy-start(bf16[1,384,4096]{2,1,0:T(8,128)(2,1)} %param.18) | copy-start | bytes 9437188
  7.2 343.8 %all-gather.3.cloned.1.call-start = ((), (), s32[]{:S(2)}) async-start(), calls=%async_computation | async-start | bytes 4718592 | tf_op jit(solution)/shard_map/all_gather | solution.py:309
  7.9 387.3 %all-gather.5.cloned.1.call-start = ((), (), s32[]{:S(2)}) async-start(), calls=%async_computation.1 | async-start | bytes 1179648 | tf_op jit(solution)/shard_map/all_gather | solution.py:314
  217.6 128.7 %copy-start.6 = (f32[128,2]{0,1:T(2,128)S(1)}, f32[128,2]{0,1:T(2,128)}, u32[]{:S(2)}) copy-start(f32[128,2]{0,1:T(2,128)} %param.15) | copy-start | bytes 3076
  346.2 2.7 copy-start.2
  346.2 2.8 copy-start.3
  349.0 2.0 copy-start.7
  351.0 4.0 copy-start.4
  351.0 4.1 %copy-start.8 = (s32[128]{0:T(128)S(1)}, s32[128]{0:T(128)}, u32[]{:S(2)}) copy-start(s32[128]{0:T(128)} %param.22) | copy-start | bytes 1540
  351.0 45.8 %copy-start.5 = (f32[512]{0:T(512)S(1)}, f32[512]{0:T(512)}, u32[]{:S(2)}) copy-start(f32[512]{0:T(512)} %param.21) | copy-start | bytes 6148
  397.2 1.3 copy-start.1
Sparse Core Ops, SparseCore 0:
  10.1 140.9 all-gather.2
  355.1 40.0 all-gather.4
